TPU v7x, 128 devices: a whole 4x4x4 slice. The times are simulated.
128 devices in a mesh: rows: 32 (over x, y, core), cols: 4 (over z).
Axes of the slice: x: 4, y: 4, z: 4, core: 2. Of those that a mesh axis runs over, the one named last changes fastest.
Arguments:
- tiles: bfloat16 [4096, 256, 256], P(('rows', 'cols')), may hold values from -15 to 20
- send_slot: int32 [128, 32], P(('rows', 'cols')), may hold values from 0 to 31, each once within a row
- slot_row: int32 [128, 32], P(('rows', 'cols')), may hold values from 0 to 2, as said below
- slot_fetch: int32 [128, 32], P(('rows', 'cols')), may hold values from 0 to 31
- fetch_list: int32 [128, 32], P(('rows', 'cols')), may hold values from 0 to 1
- basis: bfloat16 [65536, 128], P(('rows', 'cols')), may hold values from -6 to 6
Outputs:
- embedding: bfloat16 [65536, 128], P(('rows', 'cols'))
Inputs may be any that keep to these rules, and one draw needn't show every extreme that they name: `slot_row`: value 2 marks an empty slot. Within each block of 8 slots (one source builder) the filled slots come first; some device has all 32 slots filled in every draw.
All inputs are finite; a program needn't handle non-finite values.
Results may differ from a plain program's by a relative error of at most 0.02.
Values may be sent and summed in bfloat16 or wider, within the bound.
A program may use at most 128 MiB of HBM per device.

v0:
```python
import jax
import jax.numpy as jnp
from jax import lax
from jax.sharding import Mesh
from jax.sharding import PartitionSpec as P

TILE = 256
WIDTH = 128
ITERS = 6
ROWS = ("rows_0", "rows_1", "rows_2")
ROWS_COLS = ("rows_0", "rows_1", "rows_2", "cols")


def sent_to_all(shard, axis):
    count = lax.axis_size(axis)
    return lax.all_to_all(
        jnp.broadcast_to(shard[None], (count, *shard.shape)), axis, 0, 0, tiled=True
    )


def taken_together(shard, axis):
    return sent_to_all(shard, axis).sum(axis=0)


def one_axis_at_a_time(shard, axes):
    far, near = axes
    nearer = taken_together(shard, near)
    return taken_together(nearer, far)


def on_device(tiles, send_slot, slot_row, slot_fetch, fetch_list, basis):
    groups = lax.axis_size(ROWS)
    ncols = lax.axis_size("cols")
    blocks_own = basis.shape[0] // TILE
    npts = basis.shape[0] * groups * ncols
    inverse = jnp.argsort(send_slot[0])
    received = lax.all_to_all(tiles[inverse], "cols", split_axis=0, concat_axis=0, tiled=True)
    local_rows = jnp.arange(blocks_own, dtype=jnp.int32)
    one_hot = (slot_row[0][:, None] == local_rows[None, :]).astype(jnp.float32)
    row_abs = jnp.sum(jnp.abs(received.astype(jnp.float32)), axis=2)
    deg = 1.0 + jnp.dot(one_hot.T, row_abs, precision=lax.Precision.HIGHEST)
    scale = lax.rsqrt(deg).reshape(blocks_own * TILE, 1)
    wanted = fetch_list[0]
    fetch_index = slot_fetch[0]
    asked = lax.all_to_all(
        wanted.reshape(groups, 1), ROWS, split_axis=0, concat_axis=0, tiled=True
    )[:, 0]
    current = basis
    for step in range(ITERS):
        scaled = (
            (scale * current.astype(jnp.float32))
            .astype(jnp.bfloat16)
            .reshape(blocks_own, TILE, WIDTH)
        )
        arrived = lax.all_to_all(scaled[asked], ROWS, split_axis=0, concat_axis=0, tiled=True)
        chosen = arrived[fetch_index]
        prod = jnp.einsum("sak,skd->sad", received, chosen, preferred_element_type=jnp.float32)
        summed = jnp.einsum("sj,sad->jad", one_hot, prod, precision=lax.Precision.HIGHEST)
        iterate = summed.reshape(blocks_own * TILE, WIDTH) * scale
        local_gram = jnp.dot(iterate.T, iterate, precision=lax.Precision.HIGHEST)
        gram = one_axis_at_a_time(local_gram, (("rows_0", "rows_1"), ("rows_2", "cols")))
        lower = jnp.linalg.cholesky(gram / npts)
        solved = lax.linalg.triangular_solve(
            lower, iterate, left_side=False, lower=True, transpose_a=True
        )
        current = solved.astype(jnp.bfloat16)
    return current


def solution(mesh):
    split = Mesh(
        mesh.devices.reshape(4, 4, 2, mesh.shape["cols"]), ("rows_0", "rows_1", "rows_2", "cols")
    )
    return jax.shard_map(
        on_device,
        mesh=split,
        in_specs=(
            P(ROWS_COLS, None, None),
            P(ROWS_COLS, None),
            P(ROWS_COLS, None),
            P(ROWS_COLS, None),
            P(ROWS_COLS, None),
            P(ROWS_COLS, None),
        ),
        out_specs=P(ROWS_COLS, None),
        check_vma=False,
    )
```

profile of v0, /device:TPU:1, one launch (start us, length us, event | category | flops | bytes accessed | tf_op | source)
XLA Modules:
  0.0 696.8 jit_solution(922917519819048795)
XLA Ops:
  1.3 8.6 %all-to-all-start.1 = ((s32[32,1,1]{2,1,0:T(1,128)}), s32[32,1,1]{2,1,0:T(1,128)S(1)}, u32[]{:S(2)}, u32[]{:S(2)}) async-start(s32[32,1,1]{2,1,0:T(1,128)} %copy.150), calls=%async_computation.1 | async-start | bytes 32768 | tf_op jit(solution)/shard_map/all_to_all | solution.py:45
  12.3 5.0 gather_fusion
  17.3 5.2 all-to-all-start
  23.2 48.6 %all-to-all-done = bf16[32,256,256]{2,1,0:T(8,128)(2,1)} async-done(((bf16[32,256,256]{2,1,0:T(8,128)(2,1)}), bf16[32,256,256]{2,1,0:T(8,128)(2,1)}, u32[]{:S(2)}, u32[]{:S(2)}) %all-to-all-start) | async-done | bytes 4194336 | tf_op jit(solution)/shard_map/all_to_all | solution.py:37
  77.6 8.2 %all-to-all-start.2 = ((bf16[32,256,128]{2,1,0:T(8,128)(2,1)}), bf16[32,256,128]{2,1,0:T(8,128)(2,1)}, u32[]{:S(2)}, u32[]{:S(2)}) async-start(bf16[32,256,128]{2,1,0:T(8,128)(2,1)} %gather_fusion.1), calls=%async_computation.2 | async-start | bytes 4194304 | tf_op jit(solution)/shard_map/all_to_all | solution.py:55
  86.1 28.2 %all-to-all-done.2 = bf16[32,256,128]{2,1,0:T(8,128)(2,1)} async-done(((bf16[32,256,128]{2,1,0:T(8,128)(2,1)}), bf16[32,256,128]{2,1,0:T(8,128)(2,1)}, u32[]{:S(2)}, u32[]{:S(2)}) %all-to-all-start.2) | async-done | bytes 2097184 | tf_op jit(solution)/shard_map/all_to_all | solution.py:55
  120.3 3.9 broadcast_multiply_fusion.5
  124.8 12.6 %all_to_all.107 = f32[8,128,128]{2,1,0:T(8,128)S(1)} all-to-all(f32[8,128,128]{2,1,0:T(8,128)S(1)} %broadcast_in_dim.28), channel_id=1, replica_groups=mesh['rows_0'=4,'rows_1'=4,'rows_2'=2,'cols'=4] {'rows_2','cols'}, dimensions={0} | all-to-all | bytes 1048576 | tf_op jit(solution)/shard_map/all_to_all | solution.py:16
  138.5 3.8 all-to-all-start.4
  142.5 16.4 %all-to-all-done.4 = f32[16,128,128]{2,1,0:T(8,128)S(1)} async-done(((f32[16,128,128]{2,1,0:T(8,128)}), f32[16,128,128]{2,1,0:T(8,128)S(1)}, u32[]{:S(2)}, u32[]{:S(2)}) %all-to-all-start.4) | async-done | bytes 1048608 | tf_op jit(solution)/shard_map/all_to_all | solution.py:16
  159.1 11.7 %cholesky.104 = f32[128,128]{1,0:T(8,128)S(1)} custom-call(f32[128,128]{1,0:T(8,128)S(1)} %fusion.69), custom_call_target="Cholesky" | custom-call | tf_op jit(solution)/shard_map/jit(cholesky)/cholesky | solution.py:62
  172.2 9.8 %custom-call.10 = f32[1,128,128]{1,2,0:T(8,128)S(1)} custom-call(f32[1,128,128]{2,1,0:T(8,128)S(1)} %fusion.52), custom_call_target="InvertDiagBlocksLowerTriangular" | custom-call | tf_op jit(solution)/shard_map/triangular_solve/custom-call.0 | solution.py:63
  183.5 34.0 %all_to_all.108 = bf16[32,256,128]{2,1,0:T(8,128)(2,1)} all-to-all(bf16[32,256,128]{2,1,0:T(8,128)(2,1)S(1)} %gather_fusion.3), channel_id=1, replica_groups=mesh['rows_0'=4,'rows_1'=4,'rows_2'=2,'cols'=4] {'rows_0','rows_1','rows..., dimensions={0} | all-to-all | bytes 4194304 | tf_op jit(solution)/shard_map/all_to_all | solution.py:55
  223.5 3.9 broadcast_multiply_fusion.4
  228.1 11.9 %all_to_all.109 = f32[8,128,128]{2,1,0:T(8,128)S(1)} all-to-all(f32[8,128,128]{2,1,0:T(8,128)S(1)} %broadcast_in_dim.30), channel_id=1, replica_groups=mesh['rows_0'=4,'rows_1'=4,'rows_2'=2,'cols'=4] {'rows_2','cols'}, dimensions={0} | all-to-all | bytes 1048576 | tf_op jit(solution)/shard_map/all_to_all | solution.py:16
  241.1 3.9 all-to-all-start.7
  245.2 16.0 %all-to-all-done.7 = f32[16,128,128]{2,1,0:T(8,128)S(1)} async-done(((f32[16,128,128]{2,1,0:T(8,128)}), f32[16,128,128]{2,1,0:T(8,128)S(1)}, u32[]{:S(2)}, u32[]{:S(2)}) %all-to-all-start.7) | async-done | bytes 1048608 | tf_op jit(solution)/shard_map/all_to_all | solution.py:16
  261.4 11.7 %cholesky.115 = f32[128,128]{1,0:T(8,128)S(1)} custom-call(f32[128,128]{1,0:T(8,128)S(1)} %fusion.67), custom_call_target="Cholesky" | custom-call | tf_op jit(solution)/shard_map/jit(cholesky)/cholesky | solution.py:62
  274.5 9.8 %custom-call.11 = f32[1,128,128]{1,2,0:T(8,128)S(1)} custom-call(f32[1,128,128]{2,1,0:T(8,128)S(1)} %fusion.53), custom_call_target="InvertDiagBlocksLowerTriangular" | custom-call | tf_op jit(solution)/shard_map/triangular_solve/custom-call.0 | solution.py:63
  285.8 34.7 %all_to_all.110 = bf16[32,256,128]{2,1,0:T(8,128)(2,1)} all-to-all(bf16[32,256,128]{2,1,0:T(8,128)(2,1)S(1)} %gather_fusion.5), channel_id=1, replica_groups=mesh['rows_0'=4,'rows_1'=4,'rows_2'=2,'cols'=4] {'rows_0','rows_1','rows..., dimensions={0} | all-to-all | bytes 4194304 | tf_op jit(solution)/shard_map/all_to_all | solution.py:55
  326.4 3.9 broadcast_multiply_fusion.3
  331.0 11.9 %all_to_all.111 = f32[8,128,128]{2,1,0:T(8,128)S(1)} all-to-all(f32[8,128,128]{2,1,0:T(8,128)S(1)} %broadcast_in_dim.32), channel_id=1, replica_groups=mesh['rows_0'=4,'rows_1'=4,'rows_2'=2,'cols'=4] {'rows_2','cols'}, dimensions={0} | all-to-all | bytes 1048576 | tf_op jit(solution)/shard_map/all_to_all | solution.py:16
  344.0 3.8 all-to-all-start.10
  348.0 15.9 %all-to-all-done.10 = f32[16,128,128]{2,1,0:T(8,128)S(1)} async-done(((f32[16,128,128]{2,1,0:T(8,128)}), f32[16,128,128]{2,1,0:T(8,128)S(1)}, u32[]{:S(2)}, u32[]{:S(2)}) %all-to-all-start.10) | async-done | bytes 1048608 | tf_op jit(solution)/shard_map/all_to_all | solution.py:16
  364.3 11.7 %cholesky.126 = f32[128,128]{1,0:T(8,128)S(1)} custom-call(f32[128,128]{1,0:T(8,128)S(1)} %fusion.65), custom_call_target="Cholesky" | custom-call | tf_op jit(solution)/shard_map/jit(cholesky)/cholesky | solution.py:62
  377.3 9.8 %custom-call.12 = f32[1,128,128]{1,2,0:T(8,128)S(1)} custom-call(f32[1,128,128]{2,1,0:T(8,128)S(1)} %fusion.54), custom_call_target="InvertDiagBlocksLowerTriangular" | custom-call | tf_op jit(solution)/shard_map/triangular_solve/custom-call.0 | solution.py:63
  388.6 34.4 %all_to_all.112 = bf16[32,256,128]{2,1,0:T(8,128)(2,1)} all-to-all(bf16[32,256,128]{2,1,0:T(8,128)(2,1)S(1)} %gather_fusion.7), channel_id=1, replica_groups=mesh['rows_0'=4,'rows_1'=4,'rows_2'=2,'cols'=4] {'rows_0','rows_1','rows..., dimensions={0} | all-to-all | bytes 4194304 | tf_op jit(solution)/shard_map/all_to_all | solution.py:55
  425.6 3.4 fusion.98
  429.0 3.9 broadcast_multiply_fusion.2
  433.6 11.9 %all_to_all.113 = f32[8,128,128]{2,1,0:T(8,128)S(1)} all-to-all(f32[8,128,128]{2,1,0:T(8,128)S(1)} %broadcast_in_dim.34), channel_id=1, replica_groups=mesh['rows_0'=4,'rows_1'=4,'rows_2'=2,'cols'=4] {'rows_2','cols'}, dimensions={0} | all-to-all | bytes 1048576 | tf_op jit(solution)/shard_map/all_to_all | solution.py:16
  446.6 3.9 all-to-all-start.13
  450.7 15.9 %all-to-all-done.13 = f32[16,128,128]{2,1,0:T(8,128)S(1)} async-done(((f32[16,128,128]{2,1,0:T(8,128)}), f32[16,128,128]{2,1,0:T(8,128)S(1)}, u32[]{:S(2)}, u32[]{:S(2)}) %all-to-all-start.13) | async-done | bytes 1048608 | tf_op jit(solution)/shard_map/all_to_all | solution.py:16
  466.9 11.7 %cholesky.137 = f32[128,128]{1,0:T(8,128)S(1)} custom-call(f32[128,128]{1,0:T(8,128)S(1)} %fusion.63), custom_call_target="Cholesky" | custom-call | tf_op jit(solution)/shard_map/jit(cholesky)/cholesky | solution.py:62
  480.0 9.8 %custom-call.13 = f32[1,128,128]{1,2,0:T(8,128)S(1)} custom-call(f32[1,128,128]{2,1,0:T(8,128)S(1)} %fusion.55), custom_call_target="InvertDiagBlocksLowerTriangular" | custom-call | tf_op jit(solution)/shard_map/triangular_solve/custom-call.0 | solution.py:63
  491.3 34.7 %all_to_all.114 = bf16[32,256,128]{2,1,0:T(8,128)(2,1)} all-to-all(bf16[32,256,128]{2,1,0:T(8,128)(2,1)S(1)} %gather_fusion.9), channel_id=1, replica_groups=mesh['rows_0'=4,'rows_1'=4,'rows_2'=2,'cols'=4] {'rows_0','rows_1','rows..., dimensions={0} | all-to-all | bytes 4194304 | tf_op jit(solution)/shard_map/all_to_all | solution.py:55
  532.0 3.9 broadcast_multiply_fusion.1
  536.5 11.9 %all_to_all.115 = f32[8,128,128]{2,1,0:T(8,128)S(1)} all-to-all(f32[8,128,128]{2,1,0:T(8,128)S(1)} %broadcast_in_dim.36), channel_id=1, replica_groups=mesh['rows_0'=4,'rows_1'=4,'rows_2'=2,'cols'=4] {'rows_2','cols'}, dimensions={0} | all-to-all | bytes 1048576 | tf_op jit(solution)/shard_map/all_to_all | solution.py:16
  549.5 3.8 all-to-all-start.16
  553.6 15.9 %all-to-all-done.16 = f32[16,128,128]{2,1,0:T(8,128)S(1)} async-done(((f32[16,128,128]{2,1,0:T(8,128)}), f32[16,128,128]{2,1,0:T(8,128)S(1)}, u32[]{:S(2)}, u32[]{:S(2)}) %all-to-all-start.16) | async-done | bytes 1048608 | tf_op jit(solution)/shard_map/all_to_all | solution.py:16
  569.8 11.7 %cholesky.148 = f32[128,128]{1,0:T(8,128)S(1)} custom-call(f32[128,128]{1,0:T(8,128)S(1)} %fusion.61), custom_call_target="Cholesky" | custom-call | tf_op jit(solution)/shard_map/jit(cholesky)/cholesky | solution.py:62
  582.8 9.8 %custom-call.14 = f32[1,128,128]{1,2,0:T(8,128)S(1)} custom-call(f32[1,128,128]{2,1,0:T(8,128)S(1)} %fusion.56), custom_call_target="InvertDiagBlocksLowerTriangular" | custom-call | tf_op jit(solution)/shard_map/triangular_solve/custom-call.0 | solution.py:63
  594.2 34.4 %all_to_all.116 = bf16[32,256,128]{2,1,0:T(8,128)(2,1)} all-to-all(bf16[32,256,128]{2,1,0:T(8,128)(2,1)S(1)} %gather_fusion.11), channel_id=1, replica_groups=mesh['rows_0'=4,'rows_1'=4,'rows_2'=2,'cols'=4] {'rows_0','rows_1','rows..., dimensions={0} | all-to-all | bytes 4194304 | tf_op jit(solution)/shard_map/all_to_all | solution.py:55
  634.6 3.9 broadcast_multiply_fusion
  639.1 11.9 %all_to_all.117 = f32[8,128,128]{2,1,0:T(8,128)S(1)} all-to-all(f32[8,128,128]{2,1,0:T(8,128)S(1)} %broadcast_in_dim.38), channel_id=1, replica_groups=mesh['rows_0'=4,'rows_1'=4,'rows_2'=2,'cols'=4] {'rows_2','cols'}, dimensions={0} | all-to-all | bytes 1048576 | tf_op jit(solution)/shard_map/all_to_all | solution.py:16
  652.1 3.9 all-to-all-start.19
  656.2 15.9 %all-to-all-done.19 = f32[16,128,128]{2,1,0:T(8,128)S(1)} async-done(((f32[16,128,128]{2,1,0:T(8,128)}), f32[16,128,128]{2,1,0:T(8,128)S(1)}, u32[]{:S(2)}, u32[]{:S(2)}) %all-to-all-start.19) | async-done | bytes 1048608 | tf_op jit(solution)/shard_map/all_to_all | solution.py:16
  672.5 11.7 %cholesky.159 = f32[128,128]{1,0:T(8,128)S(1)} custom-call(f32[128,128]{1,0:T(8,128)S(1)} %fusion.59), custom_call_target="Cholesky" | custom-call | tf_op jit(solution)/shard_map/jit(cholesky)/cholesky | solution.py:62
  685.5 9.8 %custom-call.15 = f32[1,128,128]{1,2,0:T(8,128)S(1)} custom-call(f32[1,128,128]{2,1,0:T(8,128)S(1)} %fusion.57), custom_call_target="InvertDiagBlocksLowerTriangular" | custom-call | tf_op jit(solution)/shard_map/triangular_solve/custom-call.0 | solution.py:63
  (137 shorter events, 72.5 us)
Async XLA Ops:
  1.3 15.9 %all-to-all-start.1 = ((s32[32,1,1]{2,1,0:T(1,128)}), s32[32,1,1]{2,1,0:T(1,128)S(1)}, u32[]{:S(2)}, u32[]{:S(2)}) async-start(s32[32,1,1]{2,1,0:T(1,128)} %copy.150), calls=%async_computation.1 | async-start | bytes 32768 | tf_op jit(solution)/shard_map/all_to_all | solution.py:45
  17.3 5.2 copy-start
  17.3 54.5 %all-to-all-start = ((bf16[32,256,256]{2,1,0:T(8,128)(2,1)}), bf16[32,256,256]{2,1,0:T(8,128)(2,1)}, u32[]{:S(2)}, u32[]{:S(2)}) async-start(bf16[32,256,256]{2,1,0:T(8,128)(2,1)} %gather_fusion), calls=%async_computation | async-start | bytes 8388608 | tf_op jit(solution)/shard_map/all_to_all | solution.py:37
  23.2 51.9 %copy-start.1 = (s32[1,32]{1,0:T(1,128)S(1)}, s32[1,32]{1,0:T(1,128)}, u32[]{:S(2)}) copy-start(s32[1,32]{1,0:T(1,128)} %param.11) | copy-start | bytes 388
  77.6 8.3 %copy-start.2 = (s32[1,32]{1,0:T(1,128)S(1)}, s32[1,32]{1,0:T(1,128)}, u32[]{:S(2)}) copy-start(s32[1,32]{1,0:T(1,128)} %param.12) | copy-start | bytes 388
  77.6 36.6 %all-to-all-start.2 = ((bf16[32,256,128]{2,1,0:T(8,128)(2,1)}), bf16[32,256,128]{2,1,0:T(8,128)(2,1)}, u32[]{:S(2)}, u32[]{:S(2)}) async-start(bf16[32,256,128]{2,1,0:T(8,128)(2,1)} %gather_fusion.1), calls=%async_computation.2 | async-start | bytes 4194304 | tf_op jit(solution)/shard_map/all_to_all | solution.py:55
  138.5 20.4 %all-to-all-start.4 = ((f32[16,128,128]{2,1,0:T(8,128)}), f32[16,128,128]{2,1,0:T(8,128)S(1)}, u32[]{:S(2)}, u32[]{:S(2)}) async-start(f32[16,128,128]{2,1,0:T(8,128)} %broadcast_in_dim.29), calls=%async_computation.4 | async-start | bytes 2097152 | tf_op jit(solution)/shard_map/all_to_all | solution.py:16
  241.1 20.1 %all-to-all-start.7 = ((f32[16,128,128]{2,1,0:T(8,128)}), f32[16,128,128]{2,1,0:T(8,128)S(1)}, u32[]{:S(2)}, u32[]{:S(2)}) async-start(f32[16,128,128]{2,1,0:T(8,128)} %broadcast_in_dim.31), calls=%async_computation.7 | async-start | bytes 2097152 | tf_op jit(solution)/shard_map/all_to_all | solution.py:16
  344.0 20.0 %all-to-all-start.10 = ((f32[16,128,128]{2,1,0:T(8,128)}), f32[16,128,128]{2,1,0:T(8,128)S(1)}, u32[]{:S(2)}, u32[]{:S(2)}) async-start(f32[16,128,128]{2,1,0:T(8,128)} %broadcast_in_dim.33), calls=%async_computation.10 | async-start | bytes 2097152 | tf_op jit(solution)/shard_map/all_to_all | solution.py:16
  446.6 20.0 %all-to-all-start.13 = ((f32[16,128,128]{2,1,0:T(8,128)}), f32[16,128,128]{2,1,0:T(8,128)S(1)}, u32[]{:S(2)}, u32[]{:S(2)}) async-start(f32[16,128,128]{2,1,0:T(8,128)} %broadcast_in_dim.35), calls=%async_computation.13 | async-start | bytes 2097152 | tf_op jit(solution)/shard_map/all_to_all | solution.py:16
  549.5 20.0 %all-to-all-start.16 = ((f32[16,128,128]{2,1,0:T(8,128)}), f32[16,128,128]{2,1,0:T(8,128)S(1)}, u32[]{:S(2)}, u32[]{:S(2)}) async-start(f32[16,128,128]{2,1,0:T(8,128)} %broadcast_in_dim.37), calls=%async_computation.16 | async-start | bytes 2097152 | tf_op jit(solution)/shard_map/all_to_all | solution.py:16
  652.1 20.0 %all-to-all-start.19 = ((f32[16,128,128]{2,1,0:T(8,128)}), f32[16,128,128]{2,1,0:T(8,128)S(1)}, u32[]{:S(2)}, u32[]{:S(2)}) async-start(f32[16,128,128]{2,1,0:T(8,128)} %broadcast_in_dim.39), calls=%async_computation.19 | async-start | bytes 2097152 | tf_op jit(solution)/shard_map/all_to_all | solution.py:16
where the time goes:
time: 707 us; the launch traced here: 697 us
  blocking collectives  244 us (35%)
  waiting for transfers between devices  173 us (24%)
  other arithmetic  144 us (20%)
  matrix products  50.2 us (7%)
  starting transfers between devices  45.2 us (6%)
  local copies, waits for them, and re-layouts  39 us (6%)
    all_to_all x5, blocking collectives, on_device(): lax.all_to_all(scaled[asked], ROWS, split_axis=0, concat_axis=0, tiled=True)  172 us
    all_to_all x6, waiting for transfers between devices, sent_to_all(): lax.all_to_all(jnp.broadcast_to(shard[None], (count, *shard.shape)), axis...  96.1 us
    another operation x18, other arithmetic, on_device(): lower = jnp.linalg.cholesky(gram / npts)  74.3 us
    all_to_all x6, blocking collectives, sent_to_all(): lax.all_to_all(jnp.broadcast_to(shard[None], (count, *shard.shape)), axis...  72.1 us
    another operation x12, other arithmetic, on_device(): lax.linalg.triangular_solve(lower, iterate, left_side=False, lower=True,...  62.8 us
    all_to_all x1, waiting for transfers between devices, on_device(): lax.all_to_all(tiles[inverse], 'cols', split_axis=0, concat_axis=0, tiled...  48.6 us
    all_to_all x1, waiting for transfers between devices, on_device(): lax.all_to_all(scaled[asked], ROWS, split_axis=0, concat_axis=0, tiled=True)  28.2 us
    dot_general x6, matrix products, on_device(): jnp.einsum('sj,sad->jad', one_hot, prod, precision=lax.Precision.HIGHEST)  23.3 us
  transfers between devices with their start and end apart: 9, of which 8 were waited for; matrix products, arithmetic and copies ran while one was open for 1% of the time, Pallas kernels for 0%

commit v1 on v0

v1 whole, which is shorter than its diff:
```python
import jax
import jax.numpy as jnp
from jax import lax
from jax.experimental import pallas as pl
from jax.experimental.pallas import tpu as pltpu
from jax.sharding import Mesh
from jax.sharding import PartitionSpec as P

TILE = 256
WIDTH = 128
ITERS = 6
NX, NY, NK, NZ = 4, 4, 2, 4
Q = 8
SLOTS = NZ * Q
AXES = ("x", "y", "k", "z")
MESH = pl.DeviceIdType.MESH
HI = lax.Precision.HIGHEST
F32 = jnp.float32
BF16 = jnp.bfloat16


def contract(a, b, da, db, precision=None):
    return lax.dot_general(
        a, b, (((da,), (db,)), ((), ())), precision=precision, preferred_element_type=F32
    )


def kernel(
    meta, tiles, basis, out,
    tin, stg, recv, relay, rsend, rrecv, mrow, scale, gat_even, gat_odd, ybuf, acc,
    gram, zbuf, xbuf, vbuf, gfull, aug, linv,
    in_sem, tile_send, tile_recv, row_send, row_recv,
    ag_send, ag_own, ag_par, ar_send, zsem, xsem, ysem, fsem,
):
    x, y, k, z = (lax.axis_index(a) for a in AXES)
    mod = lax.rem
    xr, xl, xo = mod(x + 1, NX), mod(x + 3, NX), mod(x + 2, NX)
    yr, yl, yo = mod(y + 1, NY), mod(y + 3, NY), mod(y + 2, NY)
    zr, zl, zo = mod(z + 1, NZ), mod(z + 3, NZ), mod(z + 2, NZ)
    kp = 1 - k
    kz_peers = [
        (mod(k + dk, NK), mod(z + dz, NZ))
        for dk in range(NK) for dz in range(NZ) if (dk, dz) != (0, 0)
    ]
    x_peers, y_peers, z_peers = (xr, xl, xo), (yr, yl, yo), (zr, zl, zo)
    me_kz = k * NZ + z

    def remote(src, dst, ssem, rsem, **dev):
        return pltpu.make_async_remote_copy(
            src_ref=src, dst_ref=dst, send_sem=ssem, recv_sem=rsem,
            device_id=dev, device_id_type=MESH,
        )

    load_tiles = pltpu.make_async_copy(tiles, tin, in_sem)
    load_tiles.start()

    barrier = pltpu.get_barrier_semaphore()
    for pk, pz in kz_peers:
        pl.semaphore_signal(barrier, inc=1, device_id={"k": pk, "z": pz}, device_id_type=MESH)
    for px in x_peers:
        pl.semaphore_signal(barrier, inc=1, device_id={"x": px}, device_id_type=MESH)
    for py in y_peers:
        pl.semaphore_signal(barrier, inc=1, device_id={"y": py}, device_id_type=MESH)
    for s in range(SLOTS):
        for j in range(2):
            hit = jnp.where(meta[1, s] == j, 1.0, 0.0).astype(F32)
            mrow[j, s : s + 1, :] = jnp.full((1, WIDTH), hit, F32)
    load_tiles.wait()

    ones = jnp.ones((8, TILE), BF16)

    def stage(d, carry):
        for q in range(Q):
            t = tin[meta[0, d * Q + q]]
            stg[d * Q + q] = t
            rsend[d, q : q + 1, :] = contract(ones, jnp.abs(t), 1, 1)[0:1]
        return carry

    lax.fori_loop(0, NZ, stage, 0)
    pl.semaphore_wait(barrier, len(kz_peers) + len(x_peers) + len(y_peers))

    row_copies = [
        remote(rsend.at[pz], rrecv.at[z], row_send.at[i], row_recv.at[z], z=pz)
        for i, pz in enumerate(z_peers)
    ]
    for c in row_copies:
        c.start()
    half = Q // 2

    def part(start, count):
        return pl.ds(start, count)

    tile_copies = [
        remote(stg.at[part(zo * Q, half)], relay.at[0], tile_send.at[0], tile_recv.at[0], z=zr),
        remote(stg.at[part(zo * Q + half, half)], relay.at[1], tile_send.at[1], tile_recv.at[1], z=zl),
        remote(stg.at[part(zr * Q, Q)], recv.at[part(z * Q, Q)], tile_send.at[2], tile_recv.at[2], z=zr),
        remote(stg.at[part(zl * Q, Q)], recv.at[part(z * Q, Q)], tile_send.at[3], tile_recv.at[3], z=zl),
    ]
    for c in tile_copies:
        c.start()
    for q in range(Q):
        recv[z * Q + q] = stg[z * Q + q]
    rrecv[z] = rsend[z]
    for pz in z_peers:
        pltpu.make_async_copy(rrecv.at[pz], rrecv.at[pz], row_recv.at[pz]).wait()
    for c in row_copies:
        c.wait_send()
    rows = rrecv[...].reshape(SLOTS, TILE)
    for j in range(2):
        scale[j] = lax.rsqrt(1.0 + contract(rows, mrow[j], 0, 0, HI))

    gat = (gat_even, gat_odd)

    def place(flow, core, px, py):
        return ((core * 2 + flow) * NX + px) * NY + py

    def block(par, flow, px, py, piece=None, core=None):
        ref = gat[par].at[place(flow, k if core is None else core, px, py)]
        return ref if piece is None else ref.at[pl.ds(piece * (TILE // 2), TILE // 2)]

    def push(par, flow, px, py, piece=None, **dev):
        ref = block(par, flow, px, py, piece)
        remote(ref, ref, ag_send, ag_own.at[par, flow, px * NY + py], **dev).start()

    def to_partner(par, flow, px, py):
        ref = block(par, flow, px, py)
        remote(ref, ref, ag_send, ag_par.at[par, flow, px * NY + py], k=kp).start()

    def arrived(par, flow, px, py):
        ref = block(par, flow, px, py)
        pltpu.make_async_copy(ref, ref, ag_own.at[par, flow, px * NY + py]).wait()
        to_partner(par, flow, px, py)

    def oriented(flow):
        if flow == 0:
            return (x, xr, xl, xo), (y, yr, yl, yo), "x", "y"
        return (y, yr, yl, yo), (x, xr, xl, xo), "y", "x"

    def at(flow, a, b):
        return (a, b) if flow == 0 else (b, a)

    def gather_own(par):
        for flow in range(2):
            (a, ar, al, ao), (b, br, bl, bo), an, bn = oriented(flow)
            push(par, flow, *at(flow, a, b), **{an: ar})
            push(par, flow, *at(flow, a, b), **{an: al})
        for flow in range(2):
            (a, ar, al, ao), (b, br, bl, bo), an, bn = oriented(flow)
            push(par, flow, *at(flow, a, b), **{bn: br})
            push(par, flow, *at(flow, a, b), **{bn: bl})
        for flow in range(2):
            to_partner(par, flow, x, y)

    def gather_first(par):
        for flow in range(2):
            (a, ar, al, ao), (b, br, bl, bo), an, bn = oriented(flow)
            arrived(par, flow, *at(flow, al, b))
            push(par, flow, *at(flow, al, b), piece=0, **{an: ar})
            push(par, flow, *at(flow, al, b), **{bn: br})
            push(par, flow, *at(flow, al, b), **{bn: bl})
            arrived(par, flow, *at(flow, ar, b))
            push(par, flow, *at(flow, ar, b), piece=1, **{an: al})
            push(par, flow, *at(flow, ar, b), **{bn: br})
            push(par, flow, *at(flow, ar, b), **{bn: bl})

    def across(par, flow, a):
        (_, _, _, _), (b, br, bl, bo), an, bn = oriented(flow)
        arrived(par, flow, *at(flow, a, bl))
        push(par, flow, *at(flow, a, bl), piece=0, **{bn: br})
        arrived(par, flow, *at(flow, a, br))
        push(par, flow, *at(flow, a, br), piece=1, **{bn: bl})

    def gather_second(par):
        for flow in range(2):
            across(par, flow, oriented(flow)[0][0])
        for flow in range(2):
            (a, ar, al, ao), (b, br, bl, bo), an, bn = oriented(flow)
            arrived(par, flow, *at(flow, ao, b))
            push(par, flow, *at(flow, ao, b), **{bn: br})
            push(par, flow, *at(flow, ao, b), **{bn: bl})

    def gather_third(par):
        for flow in range(2):
            (a, ar, al, ao), (b, br, bl, bo), an, bn = oriented(flow)
            across(par, flow, al)
            across(par, flow, ar)
        for flow in range(2):
            (a, ar, al, ao), (b, br, bl, bo), an, bn = oriented(flow)
            arrived(par, flow, *at(flow, a, bo))

    def gather_fourth(par):
        for flow in range(2):
            across(par, flow, oriented(flow)[0][3])

    def gather_end(par):
        for flow in range(2):
            (a, ar, al, ao), (b, br, bl, bo), an, bn = oriented(flow)
            for c in (al, ar, ao):
                arrived(par, flow, *at(flow, c, bo))
        for flow in range(2):
            for px in range(NX):
                for py in range(NY):
                    ref = block(par, flow, px, py, core=kp)
                    pltpu.make_async_copy(ref, ref, ag_par.at[par, flow, px * NY + py]).wait()
        sent = gat[par].at[pl.ds(0, 62)]
        pltpu.make_async_copy(sent, sent, ag_send).wait()

    def set_basis(par, values):
        for j in range(2):
            gat[par][place(j, k, x, y)] = (scale[j] * values[j]).astype(BF16)

    def gram_send(par):
        zbuf[par, me_kz] = gram[me_kz]
        for pk, pz in kz_peers:
            remote(gram.at[pk * NZ + pz], zbuf.at[par, me_kz], ar_send.at[0], zsem.at[par, me_kz], k=pk, z=pz).start()

    def wait_for(ref, sem):
        pltpu.make_async_copy(ref, ref, sem).wait()

    def gram_x(par):
        for pk, pz in kz_peers:
            wait_for(zbuf.at[par, pk * NZ + pz], zsem.at[par, pk * NZ + pz])
        xbuf[par, x] = sum(zbuf[par, i] for i in range(1, NK * NZ)) + zbuf[par, 0]
        for px in x_peers:
            remote(xbuf.at[par, x], xbuf.at[par, x], ar_send.at[1], xsem.at[par, x], x=px).start()

    def gram_y(par):
        for px in x_peers:
            wait_for(xbuf.at[par, px], xsem.at[par, px])
        vbuf[par, y] = (xbuf[par, 0] + xbuf[par, 1]) + (xbuf[par, 2] + xbuf[par, 3])
        for py in y_peers:
            remote(vbuf.at[par, y], vbuf.at[par, y], ar_send.at[2], ysem.at[par, y], y=py).start()

    def gram_all(par):
        for py in y_peers:
            wait_for(vbuf.at[par, py], ysem.at[par, py])
        gfull[par, me_kz] = (vbuf[par, 0] + vbuf[par, 1]) + (vbuf[par, 2] + vbuf[par, 3])
        for pk, pz in kz_peers:
            remote(gfull.at[par, me_kz], gfull.at[par, me_kz], ar_send.at[3], fsem.at[par, me_kz], k=pk, z=pz).start()

    def gram_end(par):
        for pk, pz in kz_peers:
            wait_for(gfull.at[par, pk * NZ + pz], fsem.at[par, pk * NZ + pz])
        wait_for(gram.at[pl.ds(0, 7)], ar_send.at[0])
        wait_for(xbuf.at[par, pl.ds(0, 3)], ar_send.at[1])
        wait_for(vbuf.at[par, pl.ds(0, 3)], ar_send.at[2])
        wait_for(gfull.at[par, pl.ds(0, 7)], ar_send.at[3])

    sub = lax.broadcasted_iota(jnp.int32, (8, 2 * WIDTH), 0)
    npts = NX * NY * NK * NZ * 2 * TILE

    def factor(par):
        aug[:, 0:WIDTH] = gfull[par].reshape(WIDTH, WIDTH) * (1.0 / npts)
        row_id = lax.broadcasted_iota(jnp.int32, (WIDTH, WIDTH), 0)
        col_id = lax.broadcasted_iota(jnp.int32, (WIDTH, WIDTH), 1)
        aug[:, WIDTH:] = jnp.where(row_id == col_id, 1.0, 0.0).astype(F32)
        for p in range(WIDTH // 8):
            rows8 = aug[8 * p : 8 * p + 8, :]
            for j in range(8):
                lane = 8 * p + j
                col = jnp.broadcast_to(rows8[:, lane : lane + 1], (8, 2 * WIDTH))
                pivot = jnp.broadcast_to(col[j : j + 1], (8, 2 * WIDTH))
                row = jnp.broadcast_to(rows8[j : j + 1], (8, 2 * WIDTH))
                inv = lax.rsqrt(pivot)
                row = row * inv
                rows8 = jnp.where(sub > j, rows8 - (col * inv) * row, rows8)
                rows8 = jnp.where(sub == j, row, rows8)
            aug[8 * p : 8 * p + 8, :] = rows8
            if p < WIDTH // 8 - 1:
                update = contract(rows8[:, 0:WIDTH], rows8, 0, 0, HI)
                aug[8 * p + 8 :, :] = aug[8 * p + 8 :, :] - update[8 * p + 8 :, :]
        linv[...] = aug[:, WIDTH:]

    set_basis(0, basis[...].astype(F32).reshape(2, TILE, WIDTH))
    gather_own(0)
    gather_first(0)
    gather_second(0)
    gather_third(0)
    gather_fourth(0)
    for i in range(2):
        wait_for(relay.at[i], tile_recv.at[i])
    passed = [
        remote(relay.at[0], recv.at[part(zl * Q, half)], tile_send.at[4], tile_recv.at[4], z=zr),
        remote(relay.at[1], recv.at[part(zr * Q + half, half)], tile_send.at[5], tile_recv.at[5], z=zl),
    ]
    for c in passed:
        c.start()
    gather_end(0)
    linv[...] = jnp.where(
        lax.broadcasted_iota(jnp.int32, (WIDTH, WIDTH), 0)
        == lax.broadcasted_iota(jnp.int32, (WIDTH, WIDTH), 1), 1.0, 0.0,
    ).astype(F32)
    wait_for(recv.at[part(zl * Q, Q)], tile_recv.at[2])
    wait_for(recv.at[part(zr * Q, Q)], tile_recv.at[3])
    wait_for(recv.at[part(zo * Q, half)], tile_recv.at[4])
    wait_for(recv.at[part(zo * Q + half, half)], tile_recv.at[5])
    for c in tile_copies:
        c.wait_send()
    for c in passed:
        c.wait_send()

    def multiply(par):
        acc[...] = jnp.zeros_like(acc)

        def group(g, carry):
            left, right = [], []
            for q in range(Q):
                s = g * Q + q
                fetch = meta[2, s]
                where = (mod(fetch, 2) * 2 + meta[3, fetch]) * (NX * NY) + fetch // 2
                u = gat[par][where]
                row = meta[1, s]
                zero = jnp.zeros_like(u)
                left.append(recv[s])
                right.append(
                    jnp.concatenate([jnp.where(row == 0, u, zero), jnp.where(row == 1, u, zero)], axis=1)
                )
            acc[...] += jnp.dot(
                jnp.concatenate(left, axis=1), jnp.concatenate(right, axis=0),
                preferred_element_type=F32,
            )
            return carry

        lax.fori_loop(0, NZ, group, 0)

    def iteration(now, more):
        later = 1 - now
        multiply(now)
        for j in range(2):
            ybuf[j] = contract(scale[j] * acc[:, j * WIDTH : (j + 1) * WIDTH], linv[...], 1, 1, HI)
        local = contract(ybuf[0], ybuf[0], 0, 0, HI) + contract(ybuf[1], ybuf[1], 0, 0, HI)
        gram[...] = local.reshape(NK * NZ, WIDTH // (NK * NZ), WIDTH)

        def when_more(body):
            if more is True:
                body()
            else:
                pl.when(more)(body)

        when_more(lambda: set_basis(later, ybuf))
        gram_send(later)

        def first():
            gather_own(later)
            gather_first(later)

        when_more(first)
        gram_x(later)
        when_more(lambda: gather_second(later))
        gram_y(later)
        gram_all(later)

        def last():
            gather_third(later)
            gather_fourth(later)

        when_more(last)
        gram_end(later)
        factor(later)
        when_more(lambda: gather_end(later))

    def pair(i, carry):
        iteration(0, True)
        iteration(1, i < ITERS // 2 - 1)
        return carry

    lax.fori_loop(0, ITERS // 2, pair, 0)
    for j in range(2):
        out[j * TILE : (j + 1) * TILE, :] = contract(ybuf[j], linv[...], 1, 1, HI).astype(BF16)


def on_device(tiles, send_slot, slot_row, slot_fetch, fetch_list, basis):
    slots = jnp.arange(SLOTS, dtype=jnp.int32)
    hit = send_slot[0][None, :] == slots[:, None]
    inverse = jnp.sum(jnp.where(hit, slots[None, :], 0), axis=1, dtype=jnp.int32)
    meta = jnp.concatenate([inverse[None], slot_row, slot_fetch, fetch_list], axis=0)
    dma = pltpu.SemaphoreType.DMA
    vmem = pltpu.VMEM
    chunk = WIDTH // (NK * NZ)
    return pl.pallas_call(
        kernel,
        out_shape=jax.ShapeDtypeStruct(basis.shape, BF16),
        in_specs=[
            pl.BlockSpec(memory_space=pltpu.SMEM),
            pl.BlockSpec(memory_space=pl.ANY),
            pl.BlockSpec(memory_space=pltpu.VMEM),
        ],
        out_specs=pl.BlockSpec(memory_space=pltpu.VMEM),
        scratch_shapes=[
            vmem((SLOTS, TILE, TILE), BF16),
            vmem((SLOTS, TILE, TILE), BF16),
            vmem((SLOTS, TILE, TILE), BF16),
            vmem((2, Q // 2, TILE, TILE), BF16),
            vmem((NZ, Q, TILE), F32),
            vmem((NZ, Q, TILE), F32),
            vmem((2, SLOTS, WIDTH), F32),
            vmem((2, TILE, WIDTH), F32),
            vmem((2 * NX * NY * NK, TILE, WIDTH), BF16),
            vmem((2 * NX * NY * NK, TILE, WIDTH), BF16),
            vmem((2, TILE, WIDTH), F32),
            vmem((TILE, 2 * WIDTH), F32),
            vmem((NK * NZ, chunk, WIDTH), F32),
            vmem((2, NK * NZ, chunk, WIDTH), F32),
            vmem((2, NX, chunk, WIDTH), F32),
            vmem((2, NY, chunk, WIDTH), F32),
            vmem((2, NK * NZ, chunk, WIDTH), F32),
            vmem((WIDTH, 2 * WIDTH), F32),
            vmem((WIDTH, WIDTH), F32),
            dma, dma((6,)), dma((6,)), dma((NZ - 1,)), dma((NZ,)),
            dma, dma((2, 2, NX * NY)), dma((2, 2, NX * NY)),
            dma((4,)), dma((2, NK * NZ)), dma((2, NX)), dma((2, NY)), dma((2, NK * NZ)),
        ],
        compiler_params=pltpu.CompilerParams(collective_id=0, has_side_effects=True),
    )(meta, tiles, basis)


def solution(mesh):
    split = Mesh(mesh.devices.reshape(NX, NY, NK, NZ), AXES)
    return jax.shard_map(
        on_device,
        mesh=split,
        in_specs=(P(AXES, None, None),) + (P(AXES, None),) * 5,
        out_specs=P(AXES, None),
        check_vma=False,
    )
```

time: 707 us -> 310 us (0.44); the launches traced: 697 us -> 310 us
  Pallas kernels: 0 us -> 306 us
  blocking collectives: 244 us -> 0 us
  waiting for transfers between devices: 173 us -> 0 us
  other arithmetic: 144 us -> 2.05 us
  matrix products: 50.2 us -> 0 us
  starting transfers between devices: 45.2 us -> 0 us
  local copies, waits for them, and re-layouts: 39 us -> 1.57 us
    pallas_call x0 -> x1, Pallas kernels: none -> 306 us  [on_device(): pl.pallas_call(kernel, out_shape=jax.ShapeDtypeStruct(basis.shape, BF16),...]
    all_to_all x11 -> x0, blocking collectives: 244 us -> none  [the longest x5 172 us: on_device(): lax.all_to_all(scaled[asked], ROWS, split_axis=0, concat_axis=0, tiled=True)]
    all_to_all x9 -> x0, waiting for transfers between devices: 173 us -> none  [the longest x6 96.1 us: sent_to_all(): lax.all_to_all(jnp.broadcast_to(shard[None], (count, *shard.shape)), axis...]
    another operation x30 -> x0, other arithmetic: 137 us -> none  [the longest x18 74.3 us: on_device(): lower = jnp.linalg.cholesky(gram / npts)]
    dot_general x19 -> x0, matrix products: 47.6 us -> none  [the longest x6 23.3 us: on_device(): jnp.einsum('sj,sad->jad', one_hot, prod, precision=lax.Precision.HIGHEST)]
    all_to_all x9 -> x0, starting transfers between devices: 45.2 us -> none  [the longest x6 23.2 us: sent_to_all(): lax.all_to_all(jnp.broadcast_to(shard[None], (count, *shard.shape)), axis...]
    gather x13 -> x0, local copies, waits for them, and re-layouts: 27.2 us -> none  [the longest x6 15.2 us: on_device(): chosen = arrived[fetch_index]]
  transfers between devices with their start and end apart: 9 -> 0, of which waited for: 8 -> 0; matrix products, arithmetic and copies ran while one was open for 1% -> 0% of each run, Pallas kernels for 0% -> 0%
where the time goes in v1:
time: 310 us
  Pallas kernels  306 us (99%)
    pallas_call x1, Pallas kernels, on_device(): pl.pallas_call(kernel, out_shape=jax.ShapeDtypeStruct(basis.shape, BF16),...  306 us

profile of v1, /device:TPU:1, one launch (start us, length us, event | category | flops | bytes accessed | tf_op | source)
XLA Modules:
  0.0 309.9 jit_solution(13904606715503759935)
XLA Ops:
  0.0 0.8 select_reduce_fusion
  0.8 1.3 pad_add_fusion.meta
  2.0 306.3 %shard_map.64 = bf16[512,128]{1,0:T(8,128)(2,1)} custom-call(s32[4,32]{1,0:T(4,128)} %pad_add_fusion.meta, bf16[32,256,256]{2,1,0:T(8,128)(2,1)} %tiles.1, bf16[512,128]{1,0:T(8,128)(2,1)} %basis.1), custom_call_target="tpu_custom_call" | custom-call | tf_op jit(solution)/shard_map/pallas_call | solution.py:380
  308.3 1.6 copy.8

commit v2 on v1

--- a/solution.py
+++ b/solution.py
@@ -246,29 +246,62 @@
         wait_for(vbuf.at[par, pl.ds(0, 3)], ar_send.at[2])
         wait_for(gfull.at[par, pl.ds(0, 7)], ar_send.at[3])
 
-    sub = lax.broadcasted_iota(jnp.int32, (8, 2 * WIDTH), 0)
     npts = NX * NY * NK * NZ * 2 * TILE
+    panel = 16
+    lane_id = lax.broadcasted_iota(jnp.int32, (WIDTH, WIDTH), 1)
+    row_id = lax.broadcasted_iota(jnp.int32, (WIDTH, WIDTH), 0)
+    sub_id = lax.broadcasted_iota(jnp.int32, (8, WIDTH), 0)
+
+    def outer(rows):
+        high = rows.astype(BF16)
+        rest = rows - high.astype(F32)
+        mid = rest.astype(BF16)
+        low = (rest - mid.astype(F32)).astype(BF16)
+        a = jnp.concatenate([high, high, mid, mid, high, low], axis=0)
+        b = jnp.concatenate([high, mid, high, mid, low, high], axis=0)
+        return contract(a[:, 0:WIDTH], b, 0, 0)
+
+    def eliminate(base):
+        rows = [aug[pl.ds(base + r, 8, stride=0), :] for r in range(panel)]
+        d = {
+            (r, c): jnp.broadcast_to(rows[r][:, base + c : base + c + 1], (8, WIDTH))
+            for r in range(panel) for c in range(r, panel)
+        }
+        inv, low = [], {}
+        for j in range(panel):
+            inv.append(lax.rsqrt(d[j, j]))
+            for c in range(j + 1, panel):
+                low[c, j] = d[j, c] * inv[j]
+            for r in range(j + 1, panel):
+                for c in range(r, panel):
+                    d[r, c] = d[r, c] - low[r, j] * low[c, j]
+        done = []
+        for j in range(panel):
+            left, right = rows[j][:, 0:WIDTH], rows[j][:, WIDTH:]
+            for i in range(j):
+                left = left - low[j, i] * done[i][0]
+                right = right - low[j, i] * done[i][1]
+            done.append((left * inv[j], right * inv[j]))
+        groups = []
+        for o in range(0, panel, 8):
+            sides = []
+            for side in range(2):
+                v = done[o][side]
+                for j in range(1, 8):
+                    v = jnp.where(sub_id == j, done[o + j][side], v)
+                sides.append(v)
+            groups.append(jnp.concatenate(sides, axis=1))
+        return jnp.concatenate(groups, axis=0)
 
     def factor(par):
         aug[:, 0:WIDTH] = gfull[par].reshape(WIDTH, WIDTH) * (1.0 / npts)
-        row_id = lax.broadcasted_iota(jnp.int32, (WIDTH, WIDTH), 0)
-        col_id = lax.broadcasted_iota(jnp.int32, (WIDTH, WIDTH), 1)
-        aug[:, WIDTH:] = jnp.where(row_id == col_id, 1.0, 0.0).astype(F32)
-        for p in range(WIDTH // 8):
-            rows8 = aug[8 * p : 8 * p + 8, :]
-            for j in range(8):
-                lane = 8 * p + j
-                col = jnp.broadcast_to(rows8[:, lane : lane + 1], (8, 2 * WIDTH))
-                pivot = jnp.broadcast_to(col[j : j + 1], (8, 2 * WIDTH))
-                row = jnp.broadcast_to(rows8[j : j + 1], (8, 2 * WIDTH))
-                inv = lax.rsqrt(pivot)
-                row = row * inv
-                rows8 = jnp.where(sub > j, rows8 - (col * inv) * row, rows8)
-                rows8 = jnp.where(sub == j, row, rows8)
-            aug[8 * p : 8 * p + 8, :] = rows8
-            if p < WIDTH // 8 - 1:
-                update = contract(rows8[:, 0:WIDTH], rows8, 0, 0, HI)
-                aug[8 * p + 8 :, :] = aug[8 * p + 8 :, :] - update[8 * p + 8 :, :]
+        aug[:, WIDTH:] = jnp.where(row_id == lane_id, 1.0, 0.0).astype(F32)
+        for base in range(0, WIDTH, panel):
+            rows = eliminate(base)
+            aug[base : base + panel, :] = rows
+            after = base + panel
+            if after < WIDTH:
+                aug[after:, :] = aug[after:, :] - outer(rows)[after:, :]
         linv[...] = aug[:, WIDTH:]
 
     set_basis(0, basis[...].astype(F32).reshape(2, TILE, WIDTH))

time: 310 us -> 217 us (0.70)
  Pallas kernels: 306 us -> 213 us
    pallas_call x1, Pallas kernels: 306 us -> 213 us  [on_device(): pl.pallas_call(kernel, out_shape=jax.ShapeDtypeStruct(basis.shape, BF16),...]
where the time goes in v2:
time: 217 us; the launch traced here: 216 us
  Pallas kernels  213 us (98%)
    pallas_call x1, Pallas kernels, on_device(): pl.pallas_call(kernel, out_shape=jax.ShapeDtypeStruct(basis.shape, BF16),...  213 us

profile of v2, /device:TPU:1, one launch (start us, length us, event | category | flops | bytes accessed | tf_op | source)
XLA Modules:
  0.0 216.3 jit_solution(15905012960860869068)
XLA Ops:
  0.0 0.8 select_reduce_fusion
  0.8 1.3 pad_add_fusion.meta
  2.0 212.7 %shard_map.64 = bf16[512,128]{1,0:T(8,128)(2,1)} custom-call(s32[4,32]{1,0:T(4,128)} %pad_add_fusion.meta, bf16[32,256,256]{2,1,0:T(8,128)(2,1)} %tiles.1, bf16[512,128]{1,0:T(8,128)(2,1)} %basis.1), custom_call_target="tpu_custom_call" | custom-call | tf_op jit(solution)/shard_map/pallas_call | solution.py:413
  214.7 1.6 copy.8

commit v3 on v2

--- a/solution.py
+++ b/solution.py
@@ -1,3 +1,5 @@
+import functools
+
 import jax
 import jax.numpy as jnp
 from jax import lax
@@ -17,6 +19,10 @@
 HI = lax.Precision.HIGHEST
 F32 = jnp.float32
 BF16 = jnp.bfloat16
+ORDER = (
+    "basis", "send", "own", "plane", "on1", "on2", "on3", "x0", "all",
+    "x1", "x2", "x3", "sum", "factor", "last", "end",
+)
 
 
 def contract(a, b, da, db, precision=None):
@@ -28,9 +34,9 @@
 def kernel(
     meta, tiles, basis, out,
     tin, stg, recv, relay, rsend, rrecv, mrow, scale, gat_even, gat_odd, ybuf, acc,
-    gram, zbuf, xbuf, vbuf, gfull, aug, linv,
+    gram, zbuf, xybuf, gfull, aug, linv,
     in_sem, tile_send, tile_recv, row_send, row_recv,
-    ag_send, ag_own, ag_par, ar_send, zsem, xsem, ysem, fsem,
+    ag_send, ag_own, ag_par, ar_send, zsem, xysem, fsem,
 ):
     x, y, k, z = (lax.axis_index(a) for a in AXES)
     mod = lax.rem
@@ -40,9 +46,14 @@
     kp = 1 - k
     kz_peers = [
         (mod(k + dk, NK), mod(z + dz, NZ))
-        for dk in range(NK) for dz in range(NZ) if (dk, dz) != (0, 0)
+        for dz in (2, 1, 3, 0) for dk in (1, 0) if (dk, dz) != (0, 0)
     ]
-    x_peers, y_peers, z_peers = (xr, xl, xo), (yr, yl, yo), (zr, zl, zo)
+    xy_peers = [
+        (mod(x + dx, NX), mod(y + dy, NY))
+        for dx in (2, 1, 3, 0) for dy in (2, 1, 3, 0) if (dx, dy) != (0, 0)
+    ]
+    z_peers = (zo, zr, zl)
+    me_xy = x * NY + y
     me_kz = k * NZ + z
 
     def remote(src, dst, ssem, rsem, **dev):
@@ -57,10 +68,8 @@
     barrier = pltpu.get_barrier_semaphore()
     for pk, pz in kz_peers:
         pl.semaphore_signal(barrier, inc=1, device_id={"k": pk, "z": pz}, device_id_type=MESH)
-    for px in x_peers:
-        pl.semaphore_signal(barrier, inc=1, device_id={"x": px}, device_id_type=MESH)
-    for py in y_peers:
-        pl.semaphore_signal(barrier, inc=1, device_id={"y": py}, device_id_type=MESH)
+    for px, py in xy_peers:
+        pl.semaphore_signal(barrier, inc=1, device_id={"x": px, "y": py}, device_id_type=MESH)
     for s in range(SLOTS):
         for j in range(2):
             hit = jnp.where(meta[1, s] == j, 1.0, 0.0).astype(F32)
@@ -77,7 +86,7 @@
         return carry
 
     lax.fori_loop(0, NZ, stage, 0)
-    pl.semaphore_wait(barrier, len(kz_peers) + len(x_peers) + len(y_peers))
+    pl.semaphore_wait(barrier, len(kz_peers) + len(xy_peers))
 
     row_copies = [
         remote(rsend.at[pz], rrecv.at[z], row_send.at[i], row_recv.at[z], z=pz)
@@ -142,61 +151,38 @@
     def gather_own(par):
         for flow in range(2):
             (a, ar, al, ao), (b, br, bl, bo), an, bn = oriented(flow)
-            push(par, flow, *at(flow, a, b), **{an: ar})
-            push(par, flow, *at(flow, a, b), **{an: al})
+            for c in (ao, ar, al):
+                push(par, flow, *at(flow, a, b), **{an: c})
         for flow in range(2):
             (a, ar, al, ao), (b, br, bl, bo), an, bn = oriented(flow)
-            push(par, flow, *at(flow, a, b), **{bn: br})
-            push(par, flow, *at(flow, a, b), **{bn: bl})
+            for c in (br, bl):
+                push(par, flow, *at(flow, a, b), **{bn: c})
         for flow in range(2):
             to_partner(par, flow, x, y)
 
-    def gather_first(par):
-        for flow in range(2):
-            (a, ar, al, ao), (b, br, bl, bo), an, bn = oriented(flow)
-            arrived(par, flow, *at(flow, al, b))
-            push(par, flow, *at(flow, al, b), piece=0, **{an: ar})
-            push(par, flow, *at(flow, al, b), **{bn: br})
-            push(par, flow, *at(flow, al, b), **{bn: bl})
-            arrived(par, flow, *at(flow, ar, b))
-            push(par, flow, *at(flow, ar, b), piece=1, **{an: al})
-            push(par, flow, *at(flow, ar, b), **{bn: br})
-            push(par, flow, *at(flow, ar, b), **{bn: bl})
-
-    def across(par, flow, a):
-        (_, _, _, _), (b, br, bl, bo), an, bn = oriented(flow)
-        arrived(par, flow, *at(flow, a, bl))
-        push(par, flow, *at(flow, a, bl), piece=0, **{bn: br})
-        arrived(par, flow, *at(flow, a, br))
-        push(par, flow, *at(flow, a, br), piece=1, **{bn: bl})
-
-    def gather_second(par):
-        for flow in range(2):
-            across(par, flow, oriented(flow)[0][0])
-        for flow in range(2):
-            (a, ar, al, ao), (b, br, bl, bo), an, bn = oriented(flow)
-            arrived(par, flow, *at(flow, ao, b))
-            push(par, flow, *at(flow, ao, b), **{bn: br})
-            push(par, flow, *at(flow, ao, b), **{bn: bl})
-
-    def gather_third(par):
-        for flow in range(2):
-            (a, ar, al, ao), (b, br, bl, bo), an, bn = oriented(flow)
-            across(par, flow, al)
-            across(par, flow, ar)
-        for flow in range(2):
-            (a, ar, al, ao), (b, br, bl, bo), an, bn = oriented(flow)
-            arrived(par, flow, *at(flow, a, bo))
-
-    def gather_fourth(par):
-        for flow in range(2):
-            across(par, flow, oriented(flow)[0][3])
+    def onward(par, hop):
+        for flow in range(2):
+            firsts, (b, br, bl, bo), an, bn = oriented(flow)
+            arrived(par, flow, *at(flow, firsts[hop], b))
+            for c in (br, bl):
+                push(par, flow, *at(flow, firsts[hop], b), **{bn: c})
+
+    def across(par, hop):
+        for flow in range(2):
+            firsts, (b, br, bl, bo), an, bn = oriented(flow)
+            a = firsts[hop]
+            arrived(par, flow, *at(flow, a, bl))
+            push(par, flow, *at(flow, a, bl), piece=0, **{bn: br})
+            arrived(par, flow, *at(flow, a, br))
+            push(par, flow, *at(flow, a, br), piece=1, **{bn: bl})
+
+    def gather_last(par):
+        for hop in range(4):
+            for flow in range(2):
+                firsts, (b, br, bl, bo), an, bn = oriented(flow)
+                arrived(par, flow, *at(flow, firsts[hop], bo))
 
     def gather_end(par):
-        for flow in range(2):
-            (a, ar, al, ao), (b, br, bl, bo), an, bn = oriented(flow)
-            for c in (al, ar, ao):
-                arrived(par, flow, *at(flow, c, bo))
         for flow in range(2):
             for px in range(NX):
                 for py in range(NY):
@@ -209,6 +195,12 @@
         for j in range(2):
             gat[par][place(j, k, x, y)] = (scale[j] * values[j]).astype(BF16)
 
+    def total(buf, par, count):
+        terms = [buf[par, i] for i in range(count)]
+        while len(terms) > 1:
+            terms = [terms[i] + terms[i + 1] for i in range(0, len(terms), 2)]
+        return terms[0]
+
     def gram_send(par):
         zbuf[par, me_kz] = gram[me_kz]
         for pk, pz in kz_peers:
@@ -217,34 +209,28 @@
     def wait_for(ref, sem):
         pltpu.make_async_copy(ref, ref, sem).wait()
 
-    def gram_x(par):
+    def gram_plane(par):
         for pk, pz in kz_peers:
             wait_for(zbuf.at[par, pk * NZ + pz], zsem.at[par, pk * NZ + pz])
-        xbuf[par, x] = sum(zbuf[par, i] for i in range(1, NK * NZ)) + zbuf[par, 0]
-        for px in x_peers:
-            remote(xbuf.at[par, x], xbuf.at[par, x], ar_send.at[1], xsem.at[par, x], x=px).start()
-
-    def gram_y(par):
-        for px in x_peers:
-            wait_for(xbuf.at[par, px], xsem.at[par, px])
-        vbuf[par, y] = (xbuf[par, 0] + xbuf[par, 1]) + (xbuf[par, 2] + xbuf[par, 3])
-        for py in y_peers:
-            remote(vbuf.at[par, y], vbuf.at[par, y], ar_send.at[2], ysem.at[par, y], y=py).start()
+        xybuf[par, me_xy] = total(zbuf, par, NK * NZ)
+        for px, py in xy_peers:
+            mine = xybuf.at[par, me_xy]
+            remote(mine, mine, ar_send.at[1], xysem.at[par, me_xy], x=px, y=py).start()
 
     def gram_all(par):
-        for py in y_peers:
-            wait_for(vbuf.at[par, py], ysem.at[par, py])
-        gfull[par, me_kz] = (vbuf[par, 0] + vbuf[par, 1]) + (vbuf[par, 2] + vbuf[par, 3])
+        for px, py in xy_peers:
+            wait_for(xybuf.at[par, px * NY + py], xysem.at[par, px * NY + py])
+        gfull[par, me_kz] = total(xybuf, par, NX * NY)
         for pk, pz in kz_peers:
-            remote(gfull.at[par, me_kz], gfull.at[par, me_kz], ar_send.at[3], fsem.at[par, me_kz], k=pk, z=pz).start()
+            mine = gfull.at[par, me_kz]
+            remote(mine, mine, ar_send.at[2], fsem.at[par, me_kz], k=pk, z=pz).start()
 
     def gram_end(par):
         for pk, pz in kz_peers:
             wait_for(gfull.at[par, pk * NZ + pz], fsem.at[par, pk * NZ + pz])
         wait_for(gram.at[pl.ds(0, 7)], ar_send.at[0])
-        wait_for(xbuf.at[par, pl.ds(0, 3)], ar_send.at[1])
-        wait_for(vbuf.at[par, pl.ds(0, 3)], ar_send.at[2])
-        wait_for(gfull.at[par, pl.ds(0, 7)], ar_send.at[3])
+        wait_for(xybuf.at[par, pl.ds(0, 15)], ar_send.at[1])
+        wait_for(gfull.at[par, pl.ds(0, 7)], ar_send.at[2])
 
     npts = NX * NY * NK * NZ * 2 * TILE
     panel = 16
@@ -306,10 +292,11 @@
 
     set_basis(0, basis[...].astype(F32).reshape(2, TILE, WIDTH))
     gather_own(0)
-    gather_first(0)
-    gather_second(0)
-    gather_third(0)
-    gather_fourth(0)
+    for hop in (1, 2, 3):
+        onward(0, hop)
+    for hop in range(4):
+        across(0, hop)
+    gather_last(0)
     for i in range(2):
         wait_for(relay.at[i], tile_recv.at[i])
     passed = [
@@ -370,27 +357,38 @@
             else:
                 pl.when(more)(body)
 
-        when_more(lambda: set_basis(later, ybuf))
-        gram_send(later)
-
-        def first():
-            gather_own(later)
-            gather_first(later)
-
-        when_more(first)
-        gram_x(later)
-        when_more(lambda: gather_second(later))
-        gram_y(later)
-        gram_all(later)
-
-        def last():
-            gather_third(later)
-            gather_fourth(later)
-
-        when_more(last)
-        gram_end(later)
-        factor(later)
-        when_more(lambda: gather_end(later))
+        steps = {
+            "basis": lambda: set_basis(later, ybuf),
+            "own": lambda: gather_own(later),
+            "last": lambda: gather_last(later),
+            "end": lambda: gather_end(later),
+        }
+        for hop in range(4):
+            steps[f"on{hop}"] = functools.partial(onward, later, hop)
+            steps[f"x{hop}"] = functools.partial(across, later, hop)
+        sums = {
+            "send": gram_send, "plane": gram_plane, "all": gram_all, "sum": gram_end, "factor": factor,
+        }
+        waiting = []
+
+        def flush():
+            todo = list(waiting)
+            waiting.clear()
+
+            def body():
+                for name in todo:
+                    steps[name]()
+
+            if todo:
+                when_more(body)
+
+        for name in ORDER:
+            if name in sums:
+                flush()
+                sums[name](later)
+            else:
+                waiting.append(name)
+        flush()
 
     def pair(i, carry):
         iteration(0, True)
@@ -434,14 +432,13 @@
             vmem((TILE, 2 * WIDTH), F32),
             vmem((NK * NZ, chunk, WIDTH), F32),
             vmem((2, NK * NZ, chunk, WIDTH), F32),
-            vmem((2, NX, chunk, WIDTH), F32),
-            vmem((2, NY, chunk, WIDTH), F32),
+            vmem((2, NX * NY, chunk, WIDTH), F32),
             vmem((2, NK * NZ, chunk, WIDTH), F32),
             vmem((WIDTH, 2 * WIDTH), F32),
             vmem((WIDTH, WIDTH), F32),
             dma, dma((6,)), dma((6,)), dma((NZ - 1,)), dma((NZ,)),
             dma, dma((2, 2, NX * NY)), dma((2, 2, NX * NY)),
-            dma((4,)), dma((2, NK * NZ)), dma((2, NX)), dma((2, NY)), dma((2, NK * NZ)),
+            dma((3,)), dma((2, NK * NZ)), dma((2, NX * NY)), dma((2, NK * NZ)),
         ],
         compiler_params=pltpu.CompilerParams(collective_id=0, has_side_effects=True),
     )(meta, tiles, basis)

time: 217 us -> 192 us (0.88)
  Pallas kernels: 213 us -> 188 us
    pallas_call x1, Pallas kernels: 213 us -> 188 us  [on_device(): pl.pallas_call(kernel, out_shape=jax.ShapeDtypeStruct(basis.shape, BF16),...]
where the time goes in v3:
time: 192 us
  Pallas kernels  188 us (98%)
  other arithmetic  2.05 us (1%)
    pallas_call x1, Pallas kernels, on_device(): pl.pallas_call(kernel, out_shape=jax.ShapeDtypeStruct(basis.shape, BF16),...  188 us

profile of v3, /device:TPU:1, one launch (start us, length us, event | category | flops | bytes accessed | tf_op | source)
XLA Modules:
  0.0 191.6 jit_solution(8678452445001324035)
XLA Ops:
  0.0 0.8 select_reduce_fusion
  0.8 1.3 pad_add_fusion.meta
  2.0 188.0 %shard_map.64 = bf16[512,128]{1,0:T(8,128)(2,1)} custom-call(s32[4,32]{1,0:T(4,128)} %pad_add_fusion.meta, bf16[32,256,256]{2,1,0:T(8,128)(2,1)} %tiles.1, bf16[512,128]{1,0:T(8,128)(2,1)} %basis.1), custom_call_target="tpu_custom_call" | custom-call | tf_op jit(solution)/shard_map/pallas_call | solution.py:411
  190.0 1.6 copy.8

commit v4 on v3

--- a/solution.py
+++ b/solution.py
@@ -21,8 +21,9 @@
 BF16 = jnp.bfloat16
 ORDER = (
     "basis", "send", "own", "plane", "on1", "on2", "on3", "x0", "all",
-    "x1", "x2", "x3", "sum", "factor", "last", "end",
+    "x1", "x2", "x3", "sum", "top", "last", "rest", "end",
 )
+SPLIT = 80
 
 
 def contract(a, b, da, db, precision=None):
@@ -32,8 +33,8 @@
 
 
 def kernel(
-    meta, tiles, basis, out,
-    tin, stg, recv, relay, rsend, rrecv, mrow, scale, gat_even, gat_odd, ybuf, acc,
+    send_slot, slot_row, slot_fetch, fetch_list, tiles, basis, out,
+    source, tin, stg, recv, rsend, rrecv, mrow, scale, gat_even, gat_odd, ybuf, acc,
     gram, zbuf, xybuf, gfull, aug, linv,
     in_sem, tile_send, tile_recv, row_send, row_recv,
     ag_send, ag_own, ag_par, ar_send, zsem, xysem, fsem,
@@ -70,43 +71,62 @@
         pl.semaphore_signal(barrier, inc=1, device_id={"k": pk, "z": pz}, device_id_type=MESH)
     for px, py in xy_peers:
         pl.semaphore_signal(barrier, inc=1, device_id={"x": px, "y": py}, device_id_type=MESH)
+
+    def find_tile(slot, carry):
+        tile = jnp.int32(0)
+        for t in range(SLOTS):
+            tile = jnp.where(send_slot[0, t] == slot, t, tile)
+        source[slot] = tile
+        return carry
+
+    lax.fori_loop(0, SLOTS, find_tile, 0)
     for s in range(SLOTS):
         for j in range(2):
-            hit = jnp.where(meta[1, s] == j, 1.0, 0.0).astype(F32)
+            hit = jnp.where(slot_row[0, s] == j, 1.0, 0.0).astype(F32)
             mrow[j, s : s + 1, :] = jnp.full((1, WIDTH), hit, F32)
     load_tiles.wait()
 
     ones = jnp.ones((8, TILE), BF16)
 
-    def stage(d, carry):
+    def part(start, count):
+        return pl.ds(start, count)
+
+    def put_in_order(d):
         for q in range(Q):
-            t = tin[meta[0, d * Q + q]]
-            stg[d * Q + q] = t
-            rsend[d, q : q + 1, :] = contract(ones, jnp.abs(t), 1, 1)[0:1]
+            stg[d * Q + q] = tin[source[d * Q + q]]
+
+    def send_tiles(i, pz, first, count):
+        c = remote(
+            stg.at[part(pz * Q + first, count)], recv.at[part(z * Q + first, count)],
+            tile_send.at[i], tile_recv.at[z], z=pz,
+        )
+        c.start()
+        return c
+
+    few = 2
+    put_in_order(zr)
+    put_in_order(zl)
+    pl.semaphore_wait(barrier, len(kz_peers) + len(xy_peers))
+    tile_copies = [send_tiles(0, zr, 0, few), send_tiles(1, zl, 0, few)]
+    put_in_order(zo)
+    put_in_order(z)
+
+    def sum_rows(d, carry):
+        for q in range(Q):
+            t = jnp.abs(stg[d * Q + q])
+            rsend[d, q : q + 1, :] = contract(ones, t, 1, 1)[0:1]
         return carry
 
-    lax.fori_loop(0, NZ, stage, 0)
-    pl.semaphore_wait(barrier, len(kz_peers) + len(xy_peers))
-
+    lax.fori_loop(0, NZ, sum_rows, 0)
     row_copies = [
         remote(rsend.at[pz], rrecv.at[z], row_send.at[i], row_recv.at[z], z=pz)
         for i, pz in enumerate(z_peers)
     ]
     for c in row_copies:
         c.start()
-    half = Q // 2
-
-    def part(start, count):
-        return pl.ds(start, count)
-
-    tile_copies = [
-        remote(stg.at[part(zo * Q, half)], relay.at[0], tile_send.at[0], tile_recv.at[0], z=zr),
-        remote(stg.at[part(zo * Q + half, half)], relay.at[1], tile_send.at[1], tile_recv.at[1], z=zl),
-        remote(stg.at[part(zr * Q, Q)], recv.at[part(z * Q, Q)], tile_send.at[2], tile_recv.at[2], z=zr),
-        remote(stg.at[part(zl * Q, Q)], recv.at[part(z * Q, Q)], tile_send.at[3], tile_recv.at[3], z=zl),
+    tile_copies += [
+        send_tiles(2, zo, 0, Q), send_tiles(3, zr, few, Q - few), send_tiles(4, zl, few, Q - few)
     ]
-    for c in tile_copies:
-        c.start()
     for q in range(Q):
         recv[z * Q + q] = stg[z * Q + q]
     rrecv[z] = rsend[z]
@@ -279,15 +299,21 @@
             groups.append(jnp.concatenate(sides, axis=1))
         return jnp.concatenate(groups, axis=0)
 
-    def factor(par):
-        aug[:, 0:WIDTH] = gfull[par].reshape(WIDTH, WIDTH) * (1.0 / npts)
-        aug[:, WIDTH:] = jnp.where(row_id == lane_id, 1.0, 0.0).astype(F32)
-        for base in range(0, WIDTH, panel):
+    def eliminate_rows(first, last):
+        for base in range(first, last, panel):
             rows = eliminate(base)
             aug[base : base + panel, :] = rows
             after = base + panel
             if after < WIDTH:
                 aug[after:, :] = aug[after:, :] - outer(rows)[after:, :]
+
+    def factor_top(par):
+        aug[:, 0:WIDTH] = gfull[par].reshape(WIDTH, WIDTH) * (1.0 / npts)
+        aug[:, WIDTH:] = jnp.where(row_id == lane_id, 1.0, 0.0).astype(F32)
+        eliminate_rows(0, SPLIT)
+
+    def factor_rest(par):
+        eliminate_rows(SPLIT, WIDTH)
         linv[...] = aug[:, WIDTH:]
 
     set_basis(0, basis[...].astype(F32).reshape(2, TILE, WIDTH))
@@ -297,26 +323,14 @@
     for hop in range(4):
         across(0, hop)
     gather_last(0)
-    for i in range(2):
-        wait_for(relay.at[i], tile_recv.at[i])
-    passed = [
-        remote(relay.at[0], recv.at[part(zl * Q, half)], tile_send.at[4], tile_recv.at[4], z=zr),
-        remote(relay.at[1], recv.at[part(zr * Q + half, half)], tile_send.at[5], tile_recv.at[5], z=zl),
-    ]
-    for c in passed:
-        c.start()
     gather_end(0)
     linv[...] = jnp.where(
         lax.broadcasted_iota(jnp.int32, (WIDTH, WIDTH), 0)
         == lax.broadcasted_iota(jnp.int32, (WIDTH, WIDTH), 1), 1.0, 0.0,
     ).astype(F32)
-    wait_for(recv.at[part(zl * Q, Q)], tile_recv.at[2])
-    wait_for(recv.at[part(zr * Q, Q)], tile_recv.at[3])
-    wait_for(recv.at[part(zo * Q, half)], tile_recv.at[4])
-    wait_for(recv.at[part(zo * Q + half, half)], tile_recv.at[5])
+    for pz in z_peers:
+        wait_for(recv.at[part(pz * Q, Q)], tile_recv.at[pz])
     for c in tile_copies:
-        c.wait_send()
-    for c in passed:
         c.wait_send()
 
     def multiply(par):
@@ -326,10 +340,10 @@
             left, right = [], []
             for q in range(Q):
                 s = g * Q + q
-                fetch = meta[2, s]
-                where = (mod(fetch, 2) * 2 + meta[3, fetch]) * (NX * NY) + fetch // 2
+                fetch = slot_fetch[0, s]
+                where = (mod(fetch, 2) * 2 + fetch_list[0, fetch]) * (NX * NY) + fetch // 2
                 u = gat[par][where]
-                row = meta[1, s]
+                row = slot_row[0, s]
                 zero = jnp.zeros_like(u)
                 left.append(recv[s])
                 right.append(
@@ -367,7 +381,8 @@
             steps[f"on{hop}"] = functools.partial(onward, later, hop)
             steps[f"x{hop}"] = functools.partial(across, later, hop)
         sums = {
-            "send": gram_send, "plane": gram_plane, "all": gram_all, "sum": gram_end, "factor": factor,
+            "send": gram_send, "plane": gram_plane, "all": gram_all, "sum": gram_end,
+            "top": factor_top, "rest": factor_rest,
         }
         waiting = []
 
@@ -401,10 +416,6 @@
 
 
 def on_device(tiles, send_slot, slot_row, slot_fetch, fetch_list, basis):
-    slots = jnp.arange(SLOTS, dtype=jnp.int32)
-    hit = send_slot[0][None, :] == slots[:, None]
-    inverse = jnp.sum(jnp.where(hit, slots[None, :], 0), axis=1, dtype=jnp.int32)
-    meta = jnp.concatenate([inverse[None], slot_row, slot_fetch, fetch_list], axis=0)
     dma = pltpu.SemaphoreType.DMA
     vmem = pltpu.VMEM
     chunk = WIDTH // (NK * NZ)
@@ -413,15 +424,18 @@
         out_shape=jax.ShapeDtypeStruct(basis.shape, BF16),
         in_specs=[
             pl.BlockSpec(memory_space=pltpu.SMEM),
+            pl.BlockSpec(memory_space=pltpu.SMEM),
+            pl.BlockSpec(memory_space=pltpu.SMEM),
+            pl.BlockSpec(memory_space=pltpu.SMEM),
             pl.BlockSpec(memory_space=pl.ANY),
             pl.BlockSpec(memory_space=pltpu.VMEM),
         ],
         out_specs=pl.BlockSpec(memory_space=pltpu.VMEM),
         scratch_shapes=[
+            pltpu.SMEM((SLOTS,), jnp.int32),
             vmem((SLOTS, TILE, TILE), BF16),
             vmem((SLOTS, TILE, TILE), BF16),
             vmem((SLOTS, TILE, TILE), BF16),
-            vmem((2, Q // 2, TILE, TILE), BF16),
             vmem((NZ, Q, TILE), F32),
             vmem((NZ, Q, TILE), F32),
             vmem((2, SLOTS, WIDTH), F32),
@@ -436,12 +450,12 @@
             vmem((2, NK * NZ, chunk, WIDTH), F32),
             vmem((WIDTH, 2 * WIDTH), F32),
             vmem((WIDTH, WIDTH), F32),
-            dma, dma((6,)), dma((6,)), dma((NZ - 1,)), dma((NZ,)),
+            dma, dma((5,)), dma((NZ,)), dma((NZ - 1,)), dma((NZ,)),
             dma, dma((2, 2, NX * NY)), dma((2, 2, NX * NY)),
             dma((3,)), dma((2, NK * NZ)), dma((2, NX * NY)), dma((2, NK * NZ)),
         ],
         compiler_params=pltpu.CompilerParams(collective_id=0, has_side_effects=True),
-    )(meta, tiles, basis)
+    )(send_slot, slot_row, slot_fetch, fetch_list, tiles, basis)
 
 
 def solution(mesh):

time: 192 us -> 184 us (0.958)
  Pallas kernels: 188 us -> 182 us
  other arithmetic: 2.05 us -> 0 us
    pallas_call x1, Pallas kernels: 188 us -> 182 us  [on_device(): pl.pallas_call(kernel, out_shape=jax.ShapeDtypeStruct(basis.shape, BF16),...]
where the time goes in v4:
time: 184 us
  Pallas kernels  182 us (99%)
    pallas_call x1, Pallas kernels, on_device(): pl.pallas_call(kernel, out_shape=jax.ShapeDtypeStruct(basis.shape, BF16),...  182 us

profile of v4, /device:TPU:1, one launch (start us, length us, event | category | flops | bytes accessed | tf_op | source)
XLA Modules:
  0.0 183.5 jit_solution(15850060231868382916)
XLA Ops:
  0.0 182.0 %shard_map.64 = bf16[512,128]{1,0:T(8,128)(2,1)} custom-call(s32[1,32]{1,0:T(1,128)} %send_slot.1, s32[1,32]{1,0:T(1,128)} %slot_row.1, s32[1,32]{1,0:T(1,128)} %slot_fetch.1, s32[1,32]{1,0:T(1,128)} %fetch_list.1, bf16[32,256,256]{2,1,0:T(8,128)(2,1)} %tiles.1, bf16[512,128]{1,0:T(8,128)(2,1)} %basis.1), custom_call_target="tpu_custom_call" | custom-call | tf_op jit(solution)/shard_map/pallas_call | solution.py:422
  182.0 1.6 copy.8

commit v5 on v4

--- a/solution.py
+++ b/solution.py
@@ -21,9 +21,9 @@
 BF16 = jnp.bfloat16
 ORDER = (
     "basis", "send", "own", "plane", "on1", "on2", "on3", "x0", "all",
-    "x1", "x2", "x3", "sum", "top", "last", "rest", "end",
+    "x1", "x2", "x3", "sum", "top", "last", "middle",
 )
-SPLIT = 80
+SPLITS = (80, 112)
 
 
 def contract(a, b, da, db, precision=None):
@@ -310,10 +310,13 @@
     def factor_top(par):
         aug[:, 0:WIDTH] = gfull[par].reshape(WIDTH, WIDTH) * (1.0 / npts)
         aug[:, WIDTH:] = jnp.where(row_id == lane_id, 1.0, 0.0).astype(F32)
-        eliminate_rows(0, SPLIT)
+        eliminate_rows(0, SPLITS[0])
+
+    def factor_middle(par):
+        eliminate_rows(SPLITS[0], SPLITS[1])
 
     def factor_rest(par):
-        eliminate_rows(SPLIT, WIDTH)
+        eliminate_rows(SPLITS[1], WIDTH)
         linv[...] = aug[:, WIDTH:]
 
     set_basis(0, basis[...].astype(F32).reshape(2, TILE, WIDTH))
@@ -334,9 +337,8 @@
         c.wait_send()
 
     def multiply(par):
-        acc[...] = jnp.zeros_like(acc)
-
-        def group(g, carry):
+        product = None
+        for g in range(NZ):
             left, right = [], []
             for q in range(Q):
                 s = g * Q + q
@@ -349,17 +351,15 @@
                 right.append(
                     jnp.concatenate([jnp.where(row == 0, u, zero), jnp.where(row == 1, u, zero)], axis=1)
                 )
-            acc[...] += jnp.dot(
+            term = jnp.dot(
                 jnp.concatenate(left, axis=1), jnp.concatenate(right, axis=0),
                 preferred_element_type=F32,
             )
-            return carry
-
-        lax.fori_loop(0, NZ, group, 0)
+            product = term if product is None else product + term
+        acc[...] = product
 
     def iteration(now, more):
         later = 1 - now
-        multiply(now)
         for j in range(2):
             ybuf[j] = contract(scale[j] * acc[:, j * WIDTH : (j + 1) * WIDTH], linv[...], 1, 1, HI)
         local = contract(ybuf[0], ybuf[0], 0, 0, HI) + contract(ybuf[1], ybuf[1], 0, 0, HI)
@@ -375,14 +375,13 @@
             "basis": lambda: set_basis(later, ybuf),
             "own": lambda: gather_own(later),
             "last": lambda: gather_last(later),
-            "end": lambda: gather_end(later),
         }
         for hop in range(4):
             steps[f"on{hop}"] = functools.partial(onward, later, hop)
             steps[f"x{hop}"] = functools.partial(across, later, hop)
         sums = {
             "send": gram_send, "plane": gram_plane, "all": gram_all, "sum": gram_end,
-            "top": factor_top, "rest": factor_rest,
+            "top": factor_top, "middle": factor_middle,
         }
         waiting = []
 
@@ -405,11 +404,21 @@
                 waiting.append(name)
         flush()
 
+        def both():
+            gather_end(later)
+            factor_rest(later)
+            multiply(later)
+
+        when_more(both)
+        if more is not True:
+            pl.when(jnp.logical_not(more))(lambda: factor_rest(later))
+
     def pair(i, carry):
         iteration(0, True)
         iteration(1, i < ITERS // 2 - 1)
         return carry
 
+    multiply(0)
     lax.fori_loop(0, ITERS // 2, pair, 0)
     for j in range(2):
         out[j * TILE : (j + 1) * TILE, :] = contract(ybuf[j], linv[...], 1, 1, HI).astype(BF16)

time: 184 us -> 182 us (0.989)
  Pallas kernels: 182 us -> 180 us
where the time goes in v5:
time: 182 us
  Pallas kernels  180 us (99%)
    pallas_call x1, Pallas kernels, on_device(): pl.pallas_call(kernel, out_shape=jax.ShapeDtypeStruct(basis.shape, BF16),...  180 us

profile of v5, /device:TPU:1, one launch (start us, length us, event | category | flops | bytes accessed | tf_op | source)
XLA Modules:
  0.0 181.9 jit_solution(16732660299296108277)
XLA Ops:
  0.0 180.3 %shard_map.64 = bf16[512,128]{1,0:T(8,128)(2,1)} custom-call(s32[1,32]{1,0:T(1,128)} %send_slot.1, s32[1,32]{1,0:T(1,128)} %slot_row.1, s32[1,32]{1,0:T(1,128)} %slot_fetch.1, s32[1,32]{1,0:T(1,128)} %fetch_list.1, bf16[32,256,256]{2,1,0:T(8,128)(2,1)} %tiles.1, bf16[512,128]{1,0:T(8,128)(2,1)} %basis.1), custom_call_target="tpu_custom_call" | custom-call | tf_op jit(solution)/shard_map/pallas_call | solution.py:431
  180.3 1.6 copy.8

commit v6 on v5

--- a/solution.py
+++ b/solution.py
@@ -20,7 +20,7 @@
 F32 = jnp.float32
 BF16 = jnp.bfloat16
 ORDER = (
-    "basis", "send", "own", "plane", "on1", "on2", "on3", "x0", "all",
+    "basis", "own", "send", "plane", "on1", "on2", "on3", "x0", "all",
     "x1", "x2", "x3", "sum", "top", "last", "middle",
 )
 SPLITS = (80, 112)
@@ -358,12 +358,15 @@
             product = term if product is None else product + term
         acc[...] = product
 
+    def gram_local(par):
+        local = contract(ybuf[0], ybuf[0], 0, 0, HI) + contract(ybuf[1], ybuf[1], 0, 0, HI)
+        gram[...] = local.reshape(NK * NZ, WIDTH // (NK * NZ), WIDTH)
+        gram_send(par)
+
     def iteration(now, more):
         later = 1 - now
         for j in range(2):
             ybuf[j] = contract(scale[j] * acc[:, j * WIDTH : (j + 1) * WIDTH], linv[...], 1, 1, HI)
-        local = contract(ybuf[0], ybuf[0], 0, 0, HI) + contract(ybuf[1], ybuf[1], 0, 0, HI)
-        gram[...] = local.reshape(NK * NZ, WIDTH // (NK * NZ), WIDTH)
 
         def when_more(body):
             if more is True:
@@ -380,7 +383,7 @@
             steps[f"on{hop}"] = functools.partial(onward, later, hop)
             steps[f"x{hop}"] = functools.partial(across, later, hop)
         sums = {
-            "send": gram_send, "plane": gram_plane, "all": gram_all, "sum": gram_end,
+            "send": gram_local, "plane": gram_plane, "all": gram_all, "sum": gram_end,
             "top": factor_top, "middle": factor_middle,
         }
         waiting = []

time: 182 us -> 180 us (0.989)
  Pallas kernels: 180 us -> 178 us
    pallas_call x1, Pallas kernels: 180 us -> 178 us  [on_device(): pl.pallas_call(kernel, out_shape=jax.ShapeDtypeStruct(basis.shape, BF16),...]
where the time goes in v6:
time: 180 us
  Pallas kernels  178 us (99%)
    pallas_call x1, Pallas kernels, on_device(): pl.pallas_call(kernel, out_shape=jax.ShapeDtypeStruct(basis.shape, BF16),...  178 us

profile of v6, /device:TPU:1, one launch (start us, length us, event | category | flops | bytes accessed | tf_op | source)
XLA Modules:
  0.0 179.5 jit_solution(6525377301243923220)
XLA Ops:
  0.0 177.9 %shard_map.64 = bf16[512,128]{1,0:T(8,128)(2,1)} custom-call(s32[1,32]{1,0:T(1,128)} %send_slot.1, s32[1,32]{1,0:T(1,128)} %slot_row.1, s32[1,32]{1,0:T(1,128)} %slot_fetch.1, s32[1,32]{1,0:T(1,128)} %fetch_list.1, bf16[32,256,256]{2,1,0:T(8,128)(2,1)} %tiles.1, bf16[512,128]{1,0:T(8,128)(2,1)} %basis.1), custom_call_target="tpu_custom_call" | custom-call | tf_op jit(solution)/shard_map/pallas_call | solution.py:434
  177.9 1.6 copy.8
